TPU v7x, 32 devices: a whole 2x2x4 slice. The times are simulated.
32 devices in a mesh: dp: 16 (over z, y, core), tensor: 2 (over x).
Axes of the slice: x: 2, y: 2, z: 4, core: 2. Of those that a mesh axis runs over, the one named last changes fastest.
Arguments:
- hidden_in: float32 [16384, 768], P(('dp', 'tensor')), may hold values from -6 to 6
- cotangent: float32 [16384, 768], P(('dp', 'tensor')), may hold values from -6 to 6
- proj_zx: float32 [768, 2, 1536], P('dp', None, 'tensor'), may hold values from -0.21875 to 0.21875
- proj_dt: float32 [768, 24], P('dp', 'tensor'), may hold values from -0.21875 to 0.21875
- proj_bc: float32 [768, 256], P('dp'), may hold values from -0.21875 to 0.21875
- proj_out: float32 [768, 1536], P('dp', 'tensor'), may hold values from -0.15625 to 0.15625
- norm_gain: float32 [768], replicated, may hold values from 0.5 to 1.5
- conv_inner: float32 [5, 1536], P(None, 'tensor'), may hold values from -0.5 to 0.5
- conv_shared: float32 [5, 256], replicated, may hold values from -0.5 to 0.5
- head_table: float32 [3, 24], P(None, 'tensor'), may hold values from -7 to 3, as said below
- gate_gain: float32 [1536], P('tensor'), may hold values from 0.5 to 1.5
- mom_zx: float32 [768, 2, 1536], P('dp', None, 'tensor'), may hold values from -76.8 to 76.8
- mom_dt: float32 [768, 24], P('dp', 'tensor'), may hold values from -76.8 to 76.8
- mom_bc: float32 [768, 256], P('dp'), may hold values from -76.8 to 76.8
- mom_out: float32 [768, 1536], P('dp', 'tensor'), may hold values from -76.8 to 76.8
- mom_norm: float32 [768], replicated, may hold values from -76.8 to 76.8
- mom_conv: float32 [5, 1536], P(None, 'tensor'), may hold values from -76.8 to 76.8
- mom_shared: float32 [5, 256], replicated, may hold values from -76.8 to 76.8
- mom_head: float32 [3, 24], P(None, 'tensor'), may hold values from -76.8 to 76.8
- mom_gate: float32 [1536], P('tensor'), may hold values from -76.8 to 76.8
- var_zx: float32 [768, 2, 1536], P('dp', None, 'tensor'), may hold values from 16.384 to 1638.4
- var_dt: float32 [768, 24], P('dp', 'tensor'), may hold values from 16.384 to 1638.4
- var_bc: float32 [768, 256], P('dp'), may hold values from 16.384 to 1638.4
- var_out: float32 [768, 1536], P('dp', 'tensor'), may hold values from 16.384 to 1638.4
- var_norm: float32 [768], replicated, may hold values from 16.384 to 1638.4
- var_conv: float32 [5, 1536], P(None, 'tensor'), may hold values from 16.384 to 1638.4
- var_shared: float32 [5, 256], replicated, may hold values from 16.384 to 1638.4
- var_head: float32 [3, 24], P(None, 'tensor'), may hold values from 16.384 to 1638.4
- var_gate: float32 [1536], P('tensor'), may hold values from 16.384 to 1638.4
Outputs:
- hidden_out: float32 [16384, 768], P(('dp', 'tensor'))
- grad_hidden: float32 [16384, 768], P(('dp', 'tensor'))
- grad_zx: float32 [768, 2, 1536], P('dp', None, 'tensor')
- grad_dt: float32 [768, 24], P('dp', 'tensor')
- grad_bc: float32 [768, 256], P('dp')
- grad_out: float32 [768, 1536], P('dp', 'tensor')
- grad_norm: float32 [768], replicated
- grad_conv: float32 [5, 1536], P(None, 'tensor')
- grad_shared: float32 [5, 256], replicated
- grad_head: float32 [3, 24], P(None, 'tensor')
- grad_gate: float32 [1536], P('tensor')
- new_zx: float32 [768, 2, 1536], P('dp', None, 'tensor')
- new_dt: float32 [768, 24], P('dp', 'tensor')
- new_bc: float32 [768, 256], P('dp')
- new_out: float32 [768, 1536], P('dp', 'tensor')
- new_norm: float32 [768], replicated
- new_conv: float32 [5, 1536], P(None, 'tensor')
- new_shared: float32 [5, 256], replicated
- new_head: float32 [3, 24], P(None, 'tensor')
- new_gate: float32 [1536], P('tensor')
- new_mom_zx: float32 [768, 2, 1536], P('dp', None, 'tensor')
- new_mom_dt: float32 [768, 24], P('dp', 'tensor')
- new_mom_bc: float32 [768, 256], P('dp')
- new_mom_out: float32 [768, 1536], P('dp', 'tensor')
- new_mom_norm: float32 [768], replicated
- new_mom_conv: float32 [5, 1536], P(None, 'tensor')
- new_mom_shared: float32 [5, 256], replicated
- new_mom_head: float32 [3, 24], P(None, 'tensor')
- new_mom_gate: float32 [1536], P('tensor')
- new_var_zx: float32 [768, 2, 1536], P('dp', None, 'tensor')
- new_var_dt: float32 [768, 24], P('dp', 'tensor')
- new_var_bc: float32 [768, 256], P('dp')
- new_var_out: float32 [768, 1536], P('dp', 'tensor')
- new_var_norm: float32 [768], replicated
- new_var_conv: float32 [5, 1536], P(None, 'tensor')
- new_var_shared: float32 [5, 256], replicated
- new_var_head: float32 [3, 24], P(None, 'tensor')
- new_var_gate: float32 [1536], P('tensor')
Inputs may be any that keep to these rules, and one draw needn't show every extreme that they name: `head_table`: row 0 holds step size offsets, row 1 logarithms of decay rates, row 2 skip gains.
All inputs are finite; a program needn't handle non-finite values.
Results may differ from a plain program's by a relative error of at most 0.0033.
The roundings to bfloat16 on the way count: a program that leaves them out, or rounds other values in their place, can miss the bound.
Values may be sent and summed in bfloat16 or wider, within the bound.
A program may use at most 192 MiB of HBM per device.

v0:
```python
import jax
import jax.numpy as jnp
from jax import lax
from jax.sharding import PartitionSpec as P

HEADS = 24
HEAD_DIM = 64
SPAN = 256
LEN = 512
STEP = 3
INNER = 1536


epsilon = 1e-05
precise = lax.Precision.HIGHEST
beta_first = 0.9
beta_second = 0.95
learn_rate = 0.1
weight_decay = 0.01
adam_epsilon = 1e-08


def conv_silu(values, kernel, seq_count):
    kernel_taps = kernel.shape[0] - 1
    shaped = values.reshape(seq_count, LEN, values.shape[1])
    padded = jnp.pad(shaped, ((0, 0), (kernel_taps - 1, 0), (0, 0)))
    summed = kernel[kernel_taps] + jnp.zeros_like(shaped)
    for offset in range(kernel_taps):
        summed = summed + kernel[offset] * padded[:, offset : offset + LEN]
    return jax.nn.silu(summed).reshape(values.shape)


def state_space(values, step_size, decay_rate, key_rows, query_rows):
    seq_count = values.shape[0] // LEN
    blocks = LEN // SPAN
    head_count = step_size.shape[1]
    state_dim = key_rows.shape[1]
    block_x = values.reshape(seq_count, blocks, SPAN, head_count, HEAD_DIM)
    block_dt = step_size.reshape(seq_count, blocks, SPAN, head_count)
    block_b = key_rows.reshape(seq_count, blocks, SPAN, state_dim)
    block_c = query_rows.reshape(seq_count, blocks, SPAN, state_dim)
    cumul = jnp.cumsum(block_dt * decay_rate, axis=2)
    position = jnp.arange(SPAN)
    lower_mask = (position[:, None] >= position[None, :])[:, :, None]
    spread = cumul[:, :, :, None, :] - cumul[:, :, None, :, :]
    within = jnp.where(lower_mask, jnp.exp(jnp.where(lower_mask, spread, 0.0)), 0.0)
    scores = jnp.einsum("bcin,bcjn->bcij", block_c, block_b, precision=precise)
    weighted = block_x * block_dt[..., None]
    mixing_table = scores[..., None] * within
    diag_part = jnp.einsum("bcijh,bcjhp->bcihp", mixing_table, weighted, precision=precise)
    to_end = jnp.exp(cumul[:, :, -1:, :] - cumul)
    states = jnp.einsum(
        "bcjn,bcjhp->bchpn", block_b, to_end[..., None] * weighted, precision=precise
    )
    whole_decay = jnp.exp(cumul[:, :, -1, :])

    def advance(running, inputs):
        block_state, block_decay = inputs
        return (running * block_decay[:, :, None, None] + block_state, running)

    zero_state = jnp.zeros((seq_count, head_count, HEAD_DIM, state_dim), jnp.float32)
    final_state, entering = lax.scan(
        advance, zero_state, (jnp.moveaxis(states, 1, 0), jnp.moveaxis(whole_decay, 1, 0))
    )
    entering = jnp.moveaxis(entering, 0, 1)
    off_part = (
        jnp.einsum("bcin,bchpn->bcihp", block_c, entering, precision=precise)
        * jnp.exp(cumul)[..., None]
    )
    return (diag_part + off_part).reshape(seq_count * LEN, head_count * HEAD_DIM)


def mixing(x_raw, bc_raw, dt_raw, conv_inner, conv_shared, head_table):
    seq_count = x_raw.shape[0] // LEN
    x_conv = conv_silu(x_raw, conv_inner, seq_count)
    bc_conv = conv_silu(bc_raw, conv_shared, seq_count)
    state_dim = bc_raw.shape[1] // 2
    step_size = jax.nn.softplus(dt_raw + head_table[0])
    decay_rate = -jnp.exp(head_table[1])
    result = state_space(
        x_conv, step_size, decay_rate, bc_conv[:, :state_dim], bc_conv[:, state_dim:]
    )
    return result + jnp.repeat(head_table[2], HEAD_DIM) * x_conv


def adam_update(weight, moment, second, gradient):
    moment_new = beta_first * moment + (1.0 - beta_first) * gradient
    second_new = beta_second * second + (1.0 - beta_second) * gradient * gradient
    corr_first = 1.0 - beta_first**STEP
    corr_second = 1.0 - beta_second**STEP
    update = moment_new / corr_first / (jnp.sqrt(second_new / corr_second) + adam_epsilon)
    return (weight - learn_rate * (update + weight_decay * weight), moment_new, second_new)


def widen_cols(piece_part, full_cols, position):
    zero_base = jnp.zeros(piece_part.shape[:-1] + (full_cols,), jnp.float32)
    return lax.dynamic_update_slice_in_dim(
        zero_base, piece_part, position * piece_part.shape[-1], piece_part.ndim - 1
    )


def on_device(
    hidden_in,
    cotangent,
    proj_zx,
    proj_dt,
    proj_bc,
    proj_out,
    norm_gain,
    conv_inner,
    conv_shared,
    head_table,
    gate_gain,
    mom_zx,
    mom_dt,
    mom_bc,
    mom_out,
    mom_norm,
    mom_conv,
    mom_shared,
    mom_head,
    mom_gate,
    var_zx,
    var_dt,
    var_bc,
    var_out,
    var_norm,
    var_conv,
    var_shared,
    var_head,
    var_gate,
):
    tensor_pos = lax.axis_index("tensor")
    local_rows = hidden_in.shape[0]
    inner_local = proj_out.shape[1]
    heads_local = proj_dt.shape[1]
    shard_rows = proj_zx.shape[0]
    scale_in = lax.rsqrt(jnp.mean(hidden_in * hidden_in, axis=-1, keepdims=True) + epsilon)
    unit_in = hidden_in * scale_in
    normed_local = (unit_in * norm_gain).astype(jnp.bfloat16)
    normed = lax.all_gather(normed_local, "tensor", axis=0, tiled=True)
    full_zx, full_dt, full_bc, full_out = (
        lax.all_gather(proj_zx.astype(jnp.bfloat16), "dp", axis=0, tiled=True),
        lax.all_gather(proj_dt.astype(jnp.bfloat16), "dp", axis=0, tiled=True),
        lax.all_gather(proj_bc.astype(jnp.bfloat16), "dp", axis=0, tiled=True),
        lax.all_gather(proj_out.astype(jnp.bfloat16), "dp", axis=0, tiled=True),
    )
    flat_zx = full_zx.reshape(full_zx.shape[0], 2 * inner_local)
    zx_raw = jnp.dot(normed, flat_zx, preferred_element_type=jnp.float32)
    gate_pre = zx_raw[:, :inner_local]
    x_raw = zx_raw[:, inner_local:]
    bc_raw = jnp.dot(normed, full_bc, preferred_element_type=jnp.float32)
    dt_raw = jnp.dot(normed, full_dt, preferred_element_type=jnp.float32)
    mixer_out, pullback = jax.vjp(
        mixing, x_raw, bc_raw, dt_raw, conv_inner, conv_shared, head_table
    )
    gate_act = jax.nn.silu(gate_pre)
    gated_out = mixer_out * gate_act
    square_sum = lax.psum(jnp.sum(gated_out * gated_out, axis=-1), "tensor")
    scale_gate = lax.rsqrt(square_sum / INNER + epsilon)[:, None]
    unit_gate = gated_out * scale_gate
    normed_gate = (unit_gate * gate_gain).astype(jnp.bfloat16)
    cot_local = cotangent.astype(jnp.bfloat16)
    branch_out = lax.psum_scatter(
        jnp.dot(normed_gate, full_out.T, preferred_element_type=jnp.float32),
        "tensor",
        scatter_dimension=0,
        tiled=True,
    )
    cot_all = lax.all_gather(cot_local, "tensor", axis=0, tiled=True)
    d_gate_out = jnp.dot(cot_all, full_out, preferred_element_type=jnp.float32)
    grad_out_group = jnp.dot(cot_all.T, normed_gate, preferred_element_type=jnp.float32)
    hidden_out = hidden_in + branch_out
    gate_part = jnp.sum(d_gate_out * unit_gate, axis=0)
    d_unit = d_gate_out * gate_gain
    inner_dot = lax.psum(jnp.sum(d_unit * unit_gate, axis=-1), "tensor")
    d_gated = scale_gate * (d_unit - unit_gate * (inner_dot / INNER)[:, None])
    d_mixer = d_gated * gate_act
    sigm = jax.nn.sigmoid(gate_pre)
    d_gate_pre = d_gated * mixer_out * sigm * (1.0 + gate_pre * (1.0 - sigm))
    d_x_raw, d_bc_part, d_dt_raw, conv_part, shared_part, head_part = pullback(d_mixer)
    d_bc_raw = lax.psum(d_bc_part, "tensor")
    d_zx16 = jnp.concatenate([d_gate_pre, d_x_raw], axis=1).astype(jnp.bfloat16)
    d_dt16 = d_dt_raw.astype(jnp.bfloat16)
    d_bc16 = d_bc_raw.astype(jnp.bfloat16)
    partial_in = jnp.dot(d_zx16, flat_zx.T, preferred_element_type=jnp.float32)
    partial_in = partial_in + jnp.dot(d_dt16, full_dt.T, preferred_element_type=jnp.float32)
    d_normed = lax.psum_scatter(partial_in, "tensor", scatter_dimension=0, tiled=True)
    own_bc = lax.dynamic_slice_in_dim(d_bc16, tensor_pos * local_rows, local_rows, 0)
    d_normed = d_normed + jnp.dot(own_bc, full_bc.T, preferred_element_type=jnp.float32)
    zx_group = jnp.dot(normed.T, d_zx16, preferred_element_type=jnp.float32).reshape(
        flat_zx.shape[0], 2, inner_local
    )
    dt_group = jnp.dot(normed.T, d_dt16, preferred_element_type=jnp.float32)
    norm_part = jnp.sum(d_normed * unit_in, axis=0)
    d_unit_in = d_normed * norm_gain
    grad_hidden = cotangent + scale_in * (
        d_unit_in - unit_in * jnp.mean(d_unit_in * unit_in, axis=-1, keepdims=True)
    )
    wide_conv = widen_cols(conv_part, INNER, tensor_pos)
    wide_gate = widen_cols(gate_part, INNER, tensor_pos)
    wide_head = widen_cols(head_part, HEADS, tensor_pos)
    bc_own = jnp.dot(normed_local.T, own_bc, preferred_element_type=jnp.float32)
    grad_zx, grad_dt, grad_out = (
        lax.psum_scatter(zx_group, "dp", scatter_dimension=0, tiled=True),
        lax.psum_scatter(dt_group, "dp", scatter_dimension=0, tiled=True),
        lax.psum_scatter(grad_out_group, "dp", scatter_dimension=0, tiled=True),
    )
    sum_norm, sum_shared, sum_conv, sum_gate, sum_head, sum_bc = lax.psum(
        (norm_part, shared_part, wide_conv, wide_gate, wide_head, bc_own), ("dp", "tensor")
    )
    grad_bc = lax.dynamic_slice_in_dim(sum_bc, lax.axis_index("dp") * shard_rows, shard_rows, 0)
    grad_conv = lax.dynamic_slice_in_dim(sum_conv, tensor_pos * inner_local, inner_local, 1)
    grad_gate = lax.dynamic_slice_in_dim(sum_gate, tensor_pos * inner_local, inner_local, 0)
    grad_head = lax.dynamic_slice_in_dim(sum_head, tensor_pos * heads_local, heads_local, 1)
    grads = (
        grad_zx,
        grad_dt,
        grad_bc,
        grad_out,
        sum_norm,
        grad_conv,
        sum_shared,
        grad_head,
        grad_gate,
    )
    weights = (
        proj_zx,
        proj_dt,
        proj_bc,
        proj_out,
        norm_gain,
        conv_inner,
        conv_shared,
        head_table,
        gate_gain,
    )
    moments = (mom_zx, mom_dt, mom_bc, mom_out, mom_norm, mom_conv, mom_shared, mom_head, mom_gate)
    seconds = (var_zx, var_dt, var_bc, var_out, var_norm, var_conv, var_shared, var_head, var_gate)
    results = [
        adam_update(w_item, m_item, v_item, g_item)
        for w_item, m_item, v_item, g_item in zip(weights, moments, seconds, grads)
    ]
    new_weights = tuple((item[0] for item in results))
    new_moments = tuple((item[1] for item in results))
    new_seconds = tuple((item[2] for item in results))
    return (hidden_out, grad_hidden) + grads + new_weights + new_moments + new_seconds


def solution(mesh):
    placed = (
        P(("dp", "tensor"), None),
        P(("dp", "tensor"), None),
        P("dp", None, "tensor"),
        P("dp", "tensor"),
        P("dp", None),
        P("dp", "tensor"),
        P(),
        P(None, "tensor"),
        P(),
        P(None, "tensor"),
        P("tensor"),
        P("dp", None, "tensor"),
        P("dp", "tensor"),
        P("dp", None),
        P("dp", "tensor"),
        P(),
        P(None, "tensor"),
        P(),
        P(None, "tensor"),
        P("tensor"),
        P("dp", None, "tensor"),
        P("dp", "tensor"),
        P("dp", None),
        P("dp", "tensor"),
        P(),
        P(None, "tensor"),
        P(),
        P(None, "tensor"),
        P("tensor"),
    )
    return jax.shard_map(
        on_device,
        mesh=mesh,
        in_specs=placed,
        out_specs=(
            P(("dp", "tensor"), None),
            P(("dp", "tensor"), None),
            P("dp", None, "tensor"),
            P("dp", "tensor"),
            P("dp", None),
            P("dp", "tensor"),
            P(),
            P(None, "tensor"),
            P(),
            P(None, "tensor"),
            P("tensor"),
            P("dp", None, "tensor"),
            P("dp", "tensor"),
            P("dp", None),
            P("dp", "tensor"),
            P(),
            P(None, "tensor"),
            P(),
            P(None, "tensor"),
            P("tensor"),
            P("dp", None, "tensor"),
            P("dp", "tensor"),
            P("dp", None),
            P("dp", "tensor"),
            P(),
            P(None, "tensor"),
            P(),
            P(None, "tensor"),
            P("tensor"),
            P("dp", None, "tensor"),
            P("dp", "tensor"),
            P("dp", None),
            P("dp", "tensor"),
            P(),
            P(None, "tensor"),
            P(),
            P(None, "tensor"),
            P("tensor"),
        ),
        check_vma=False,
    )
```

profile of v0, /device:TPU:0, one launch (start us, length us, event | category | flops | bytes accessed | tf_op | source)
XLA Modules:
  0.0 886.6 jit_solution(6448583615369308812)
XLA Ops:
  14.2 23.3 %all-gather = bf16[16,48,12]{1,2,0:T(8,128)(2,1)S(1)} all-gather(bf16[1,48,12]{1,2,0:T(8,128)(2,1)S(1)} %convert_bitcast_fusion), channel_id=1, replica_groups=mesh['dp'=16,'tensor'=2] {'dp'}, dimensions={0}, use_global_device_ids=true | all-gather | bytes 19584 | tf_op jit(solution)/shard_map/all_gather | solution.py:144
  38.3 20.0 %all_gather.21 = bf16[768,256]{1,0:T(8,128)(2,1)} all-gather(bf16[48,256]{1,0:T(8,128)(2,1)S(1)} %convert_element_type.35), channel_id=1, replica_groups=mesh['dp'=16,'tensor'=2] {'dp'}, dimensions={0}, use_global_device_ids=true | all-gather | bytes 417792 | tf_op jit(solution)/shard_map/all_gather | solution.py:145
  73.0 13.7 %all-gather.8.cloned.1.call-done = bf16[768,2,768]{2,1,0:T(2,128)(2,1)} async-done(((bf16[48,2,768]{2,1,0:T(2,128)(2,1)}), bf16[768,2,768]{2,1,0:T(2,128)(2,1)}) %all-gather.8.cloned.1.call-update) | async-done | bytes 2359312 | tf_op jit(solution)/shard_map/all_gather | solution.py:143
  98.9 9.0 %fusion.29 = (f32[2,512,768]{1,2,0:T(8,128)}, f32[2,512,768]{1,2,0:T(8,128)}) fusion(f32[2,512,768]{1,2,0:T(8,128)} %copy.302, f32[768]{0:T(1024)S(1)} %copy-done.54, f32[768]{0:T(1024)S(1)} %get-tuple-element.591, f32[768]{0:T(1024)S(1)} %get-tuple-element.592, f32[768]{0:T(1024)S(1)} %get-tuple-element.593, f32[768]{0:T(1024)S(1)} %copy-done.72), kind=kLoop, calls=%fused_computation.66 | loop fusion | flops 9437184 | bytes 9452544 | tf_op jit(solution)/shard_map/jvp(jit(silu))/mul | solution.py:30
  116.6 6.0 fusion.57
  132.6 14.3 %bitcast_add_fusion.3 = f32[2,2,256,12,64]{2,4,3,1,0:T(8,128)S(1)} fusion(f32[2,2,256,12,64]{2,4,3,1,0:T(8,128)S(1)} %fusion.64, f32[2,2,256,12]{2,3,1,0:T(8,128)S(1)} %bitcast.239, f32[2,2,256,256]{3,2,1,0:T(8,128)S(1)} %copy-done.26, pred[256,256]{1,0:T(8,128)(4,1)S(1)} %copy-done.47, f32[2,2,256,12,64]{2,1,4,3,0:T(2,128)S(1)} %copy-done.2, ...), kind=kOutput, calls=%fused_computation.48 | convolution fusion | flops 2430861312 | bytes 10698752 | tf_op jit(solution)/shard_map/jvp(bcijh,bcjhp->bcihp)/dot_general | solution.py:50
  151.0 5.5 reshape.299
  160.0 6.4 multiply_reduce_fusion.9
  171.4 5.3 convolution_bitcast_fusion
  179.9 62.1 %reduce-scatter.15.cloned.1.call-done = f32[48,768]{1,0:T(8,128)} async-done(((f32[768,768]{1,0:T(8,128)}), f32[48,768]{1,0:T(8,128)}) %reduce-scatter.15.cloned.1.call-update) | async-done | bytes 147472
  243.9 38.2 %all-gather.10.cloned.1.call-done = bf16[768,768]{1,0:T(8,128)(2,1)} async-done(((bf16[48,768]{1,0:T(8,128)(2,1)}), bf16[768,768]{1,0:T(8,128)(2,1)}) %all-gather.10.cloned.1.call-update) | async-done | bytes 1179664 | tf_op jit(solution)/shard_map/all_gather | solution.py:146
  282.1 6.5 multiply_reduce_fusion
  288.6 5.6 psum.64
  294.9 8.9 %fusion.27 = (f32[768]{0:T(1024)}, f32[1024,768]{1,0:T(8,128)}, bf16[1024,768]{1,0:T(8,128)(2,1)}) fusion(f32[2,512,768]{2,1,0:T(8,128)} %copy.316, f32[1024,1536]{1,0:T(8,128)} %copy-done.5, f32[1024]{0:T(1024)S(1)} %broadcast_multiply_fusion.9, f32[1024,768]{1,0:T(8,128)} %get-tuple-element.665, f32[1024,768]{1,0:T(8,128)} %get-tuple-element.703, ...), kind=kLoop, calls=%fused_computation.47 | loop fusion | flops 16514304 | bytes 20464640 | tf_op jit(solution)/shard_map/transpose(jvp())/reduce_sum | solution.py:83
  307.4 5.6 reshape.301
  321.8 6.0 fusion.66
  329.7 9.1 %while.35 = (s32[]{:T(128)}, f32[2,12,64,128]{3,2,1,0:T(8,128)S(1)}, f32[2,2,12,64,128]{4,3,2,1,0:T(8,128)}, f32[2,2,12]{2,0,1:T(2,128)}, f32[2,2,12,64,128]{4,3...) while((s32[]{:T(128)}, ...), condition=%wide.region_12.13_spmd.clone, body=%wide.region_10.12_spmd.clone.sunk | while | flops 1179628 | bytes 4719300 | solution.py:62
  343.3 5.9 fusion.69
  349.2 19.4 %fusion.12 = (f32[2,2,256,12]{2,3,1,0:T(8,128)}, f32[2,2,256,12]{2,3,1,0:T(8,128)}, f32[2,2,256,256]{3,2,1,0:T(8,128)S(1)}) fusion(f32[2,2,256,12]{2,3,1,0:T(8,128)S(1)} %bitcast.240, f32[2,2,256,256]{3,2,1,0:T(8,128)S(1)} %copy-done.27, pred[256,256]{1,0:T(8,128)(4,1)S(1)} %copy-done.48, f32[2,2,256,12,64]{2,1,4,3,0:T(2,128)S(1)} %copy-done.3, ...), kind=kOutput, calls=%fused_computation.21 | convolution fusion | flops 2451021824 | bytes 8650752 | tf_op jit(solution)/shard_map/transpose(jvp(bcijh,bcjhp->bcihp))/dot_general | solution.py:50
  368.6 13.6 %multiply_reduce_fusion.5 = (f32[2,2,256,12]{2,3,1,0:T(8,128)S(1)}, f32[2,2,256,12]{2,3,1,0:T(8,128)}, f32[2,2,256,12,64]{2,4,3,1,0:T(8,128)}) fusion(f32[2,2,256,12,64]{2,4,3,1,0:T(8,128)S(1)} %fusion.61, f32[2,2,256,12,64]{2,1,4,3,0:T(2,128)S(1)} %copy-done.3, f32[2,2,256,12]{2,3,1,0:T(8,128)S(1)} %copy-done.30, f32[2,2,256,12]{2,3,1,0:T(8,128)S(1)} %bitcast.241, ...), kind=kOutput, calls=%fused_computation.54 | convolution fusion | flops 2434768896 | bytes 13942784 | tf_op jit(solution)/shard_map/transpose(jvp(bcijh,bcjhp->bcihp))/dot_general | solution.py:50
  385.8 9.9 %reduce-window.16 = f32[2,2,12,2,128]{4,2,3,1,0:T(8,128)S(1)} reduce-window(f32[2,2,12,2,128]{4,2,3,1,0:T(8,128)S(1)} %copy.337, f32[]{:T(128)} %constant.87.clone.1), window={size=1x1x1x1x128 pad=0_0x0_0x0_0x0_0x0_127}, to_apply=%region_19.20 | reduce-window | flops 1560576 | bytes 98308 | tf_op jit(solution)/shard_map/reduce-window.2
  408.6 5.5 reshape.302
  429.8 27.6 %all-reduce.36 = bf16[1024,256]{1,0:T(8,128)(2,1)S(1)} all-reduce(f32[1024,256]{1,0:T(8,128)S(1)} %bitcast.230), channel_id=1, replica_groups=mesh['dp'=16,'tensor'=2] {'tensor'}, use_global_device_ids=true, to_apply=%region_23.24 | all-reduce | flops 262144 | bytes 1572864 | tf_op jit(solution)/shard_map/psum | solution.py:182
  457.4 9.9 %multiply_reduce_fusion.4 = (f32[768]{0:T(1024)}, f32[768]{0:T(1024)S(1)}, f32[768]{0:T(1024)}, f32[768]{0:T(1024)}, f32[768]{0:T(1024)S(1)}, /*index=5*/f32[2,512,768]{1,2,0:T(8,128)S(1)}) fusion(f32[2,512,768]{1,2,0:T(8,128)} %copy.302, f32[2,512,768]{1,2,0:T(8,128)} %get-tuple-element.667, f32[2,512,768]{1,2,0:T(8,128)} %copy.325), kind=kLoop, calls=%fused_computation.53 | loop fusion | flops 14151936 | bytes 12598272 | tf_op jit(solution)/shard_map/transpose(jvp())/reduce_sum | solution.py:29
  475.3 8.4 fusion.25
  486.3 6.2 fusion.39
  492.5 6.6 reshape.313
  521.2 7.1 reduce-scatter.13.cloned.1.call-done
  531.1 131.4 %all-reduce.33.cloned.1.call-done = f32[768,256]{1,0:T(8,128)} async-done(((f32[768,256]{1,0:T(8,128)}), f32[768,256]{1,0:T(8,128)}) %all-reduce.33.cloned.1.call-update) | async-done | bytes 786448 | tf_op jit(solution)/shard_map/psum | solution.py:209
  664.0 118.0 %all-reduce.35.cloned.1.call-done = f32[768,2,768]{2,1,0:T(2,128)} async-done(((f32[768,2,768]{2,1,0:T(2,128)}), f32[768,2,768]{2,1,0:T(2,128)}) %all-reduce.35.cloned.1.call-update) | async-done | bytes 4718608
  785.1 42.4 %reduce-scatter.11.cloned.1.call-done = f32[512,768]{1,0:T(8,128)} async-done(((f32[1024,768]{1,0:T(8,128)}), f32[512,768]{1,0:T(8,128)}) %reduce-scatter.11.cloned.1.call-update) | async-done | bytes 1572880 | tf_op jit(solution)/shard_map/reduce_scatter | solution.py:188
  830.6 41.4 %all-reduce.28 = (f32[768]{0:T(1024)S(1)}, f32[5,1536]{1,0:T(8,128)S(1)}, f32[5,256]{1,0:T(8,128)S(1)}, f32[3,24]{1,0:T(4,128)S(1)}, f32[1536]{0:T(1024)S(1)}) all-reduce(f32[768]{0:T(1024)S(1)} %get-tuple-element.577, f32[5,1536]{1,0:T(8,128)S(1)} %add_dynamic-update-slice_fusion, ...), channel_id=1, replica_groups=mesh['dp'=16,'tensor'=2] {'dp','tensor'}, use_global_device_ids=true, to_apply=%region_30.31 | all-reduce | flops 11336 | bytes 90688 | tf_op jit(solution)/shard_map/psum | solution.py:209
  (376 shorter events, 183.6 us)
Async XLA Ops:
  7.2 51.8 %all-gather.6.cloned.1.call-start = ((), (), s32[]{:S(2)}) async-start(), calls=%async_computation.4 | async-start | bytes 2359296 | tf_op jit(solution)/shard_map/all_gather | solution.py:141
  11.6 75.1 %all-gather.8.cloned.1.call-start = ((), (), s32[]{:S(2)}) async-start(), calls=%async_computation.5 | async-start | bytes 2506752 | tf_op jit(solution)/shard_map/all_gather | solution.py:143
  12.4 159.0 %all-gather.12.cloned.1.call-start = ((), (), s32[]{:S(2)}) async-start(), calls=%async_computation.8 | async-start | bytes 2359296 | tf_op jit(solution)/shard_map/all_gather | solution.py:170
  13.5 228.5 %reduce-scatter.15.cloned.1.call-start = ((), (), s32[]{:S(2)}) async-start(), calls=%async_computation.12 | async-start | bytes 2506752
  171.4 123.5 %copy-start.56 = (f32[1024]{0:T(1024)}, f32[1024]{0:T(1024)S(1)}, u32[]{:S(2)}) copy-start(f32[1024]{0:T(1024)S(1)} %add_rsqrt_fusion) | copy-start | bytes 12292
  179.9 102.2 %all-gather.10.cloned.1.call-start = ((), (), s32[]{:S(2)}) async-start(), calls=%async_computation.6 | async-start | bytes 1253376 | tf_op jit(solution)/shard_map/all_gather | solution.py:146
  243.8 284.5 %reduce-scatter.13.cloned.1.call-start = ((), (), s32[]{:S(2)}) async-start(), calls=%async_computation.11 | async-start | bytes 417792
  473.9 188.6 %all-reduce.33.cloned.1.call-start = ((), (), s32[]{:S(2)}) async-start(), calls=%async_computation.10 | async-start | bytes 1572864 | tf_op jit(solution)/shard_map/psum | solution.py:209
  486.3 295.7 %all-reduce.35.cloned.1.call-start = ((), (), s32[]{:S(2)}) async-start(), calls=%async_computation.13 | async-start | bytes 9437184
  499.2 328.3 %reduce-scatter.11.cloned.1.call-start = ((), (), s32[]{:S(2)}) async-start(), calls=%async_computation.9 | async-start | bytes 4718592 | tf_op jit(solution)/shard_map/reduce_scatter | solution.py:188
  507.7 367.2 %reduce-scatter.9.cloned.1.call-start = ((), (), s32[]{:S(2)}) async-start(), calls=%async_computation.7 | async-start | bytes 4718592 | tf_op jit(solution)/shard_map/reduce_scatter | solution.py:164
  514.1 148.4 %copy-start.42 = (f32[48,256]{1,0:T(8,128)S(1)}, f32[48,256]{1,0:T(8,128)}, u32[]{:S(2)}) copy-start(f32[48,256]{1,0:T(8,128)} %param.37) | copy-start | bytes 147460
  514.1 148.4 %copy-start.51 = (f32[48,256]{1,0:T(8,128)S(1)}, f32[48,256]{1,0:T(8,128)}, u32[]{:S(2)}) copy-start(f32[48,256]{1,0:T(8,128)} %param.46) | copy-start | bytes 147460
  514.1 267.9 %copy-start.24 = (f32[48,2,768]{2,1,0:T(2,128)S(1)}, f32[48,2,768]{2,1,0:T(2,128)}, u32[]{:S(2)}) copy-start(f32[48,2,768]{2,1,0:T(2,128)} %param.35) | copy-start | bytes 884740
  514.1 267.9 %copy-start.35 = (f32[48,2,768]{2,1,0:T(2,128)S(1)}, f32[48,2,768]{2,1,0:T(2,128)}, u32[]{:S(2)}) copy-start(f32[48,2,768]{2,1,0:T(2,128)} %param.44) | copy-start | bytes 884740
  514.1 267.9 %copy-start.36 = (f32[48,2,768]{2,1,0:T(2,128)S(1)}, f32[48,2,768]{2,1,0:T(2,128)}, u32[]{:S(2)}) copy-start(f32[48,2,768]{2,1,0:T(2,128)} %param.53) | copy-start | bytes 884740
  514.1 313.4 %copy-start.4 = (f32[512,768]{1,0:T(8,128)S(1)}, f32[512,768]{1,0:T(8,128)}, u32[]{:S(2)}) copy-start(f32[512,768]{1,0:T(8,128)} %param.33) | copy-start | bytes 4718596
  514.1 313.4 %copy-start.19 = (bf16[768,256]{1,0:T(8,128)(2,1)S(1)}, bf16[768,256]{1,0:T(8,128)(2,1)}, u32[]{:S(2)}) copy-start(bf16[768,256]{1,0:T(8,128)(2,1)} %all_gather.21) | copy-start | bytes 1179652
  514.1 313.4 %copy-start.46 = (f32[768]{0:T(1024)S(1)}, f32[768]{0:T(1024)}, u32[]{:S(2)}) copy-start(f32[768]{0:T(1024)} %param.39) | copy-start | bytes 9220
  785.0 87.2 %copy-start.104 = (f32[3,12]{1,0:T(4,128)S(1)}, f32[3,12]{1,0:T(4,128)}, u32[]{:S(2)}) copy-start(f32[3,12]{1,0:T(4,128)} %param.51) | copy-start | bytes 436
  785.0 87.2 %copy-start.105 = (f32[3,12]{1,0:T(4,128)S(1)}, f32[3,12]{1,0:T(4,128)}, u32[]{:S(2)}) copy-start(f32[3,12]{1,0:T(4,128)} %param.60) | copy-start | bytes 436
  785.0 87.9 %copy-start.70 = (f32[5,256]{1,0:T(8,128)S(1)}, f32[5,256]{1,0:T(8,128)}, u32[]{:S(2)}) copy-start(f32[5,256]{1,0:T(8,128)} %param.41) | copy-start | bytes 15364
  785.0 87.9 %copy-start.84 = (f32[5,256]{1,0:T(8,128)S(1)}, f32[5,256]{1,0:T(8,128)}, u32[]{:S(2)}) copy-start(f32[5,256]{1,0:T(8,128)} %param.50) | copy-start | bytes 15364
  785.0 87.8 %copy-start.85 = (f32[5,256]{1,0:T(8,128)S(1)}, f32[5,256]{1,0:T(8,128)}, u32[]{:S(2)}) copy-start(f32[5,256]{1,0:T(8,128)} %param.59) | copy-start | bytes 15364
  785.0 88.5 %copy-start.99 = (f32[768]{0:T(1024)S(1)}, f32[768]{0:T(1024)}, u32[]{:S(2)}) copy-start(f32[768]{0:T(1024)} %param.52) | copy-start | bytes 9220
  785.0 88.5 %copy-start.100 = (f32[768]{0:T(1024)S(1)}, f32[768]{0:T(1024)}, u32[]{:S(2)}) copy-start(f32[768]{0:T(1024)} %param.61) | copy-start | bytes 9220
  785.0 88.4 %copy-start.101 = (f32[768]{0:T(1024)S(1)}, f32[768]{0:T(1024)}, u32[]{:S(2)}) copy-start(f32[768]{0:T(1024)} %param.57) | copy-start | bytes 9220
  785.1 88.4 %copy-start.102 = (f32[768]{0:T(1024)S(1)}, f32[768]{0:T(1024)}, u32[]{:S(2)}) copy-start(f32[768]{0:T(1024)} %param.48) | copy-start | bytes 9220
  785.1 89.1 %copy-start.50 = (f32[5,768]{1,0:T(8,128)S(1)}, f32[5,768]{1,0:T(8,128)}, u32[]{:S(2)}) copy-start(f32[5,768]{1,0:T(8,128)} %param.40) | copy-start | bytes 46084
  785.1 89.1 %copy-start.67 = (f32[5,768]{1,0:T(8,128)S(1)}, f32[5,768]{1,0:T(8,128)}, u32[]{:S(2)}) copy-start(f32[5,768]{1,0:T(8,128)} %param.49) | copy-start | bytes 46084
  785.1 89.1 %copy-start.68 = (f32[5,768]{1,0:T(8,128)S(1)}, f32[5,768]{1,0:T(8,128)}, u32[]{:S(2)}) copy-start(f32[5,768]{1,0:T(8,128)} %param.58) | copy-start | bytes 46084
  785.1 89.8 %copy-start.65 = (f32[512]{0:T(512)S(1)}, f32[512]{0:T(512)}, u32[]{:S(2)}) copy-start(f32[512]{0:T(512)} %copy-done.64) | copy-start | bytes 6148
  (86 other events, 989.1 us)
Sparse Core Ops, SparseCore 0:
  11.7 29.8 all-gather.5
  44.5 42.1 all-gather.7
  88.8 25.8 all-gather.11
  180.0 61.9 reduce-scatter.14
  244.7 37.3 all-gather.9
  474.0 54.2 reduce-scatter.12
  533.5 128.9 all-reduce.32
  666.1 115.8 all-reduce.34
  784.3 43.1 reduce-scatter.10
  829.6 44.7 reduce-scatter.8
where the time goes:
time: 898 us; the launch traced here: 887 us
  waiting for transfers between devices  413 us (46%)
  matrix products  129 us (14%)
  blocking collectives  123 us (14%)
  other arithmetic  110 us (12%)
  local copies, waits for them, and re-layouts  93.6 us (10%)
  between operations  16.5 us (2%)
    unnamed x13, waiting for transfers between devices  187 us
    psum x1, waiting for transfers between devices, on_device(): lax.psum((norm_part, shared_part, wide_conv, wide_gate, wide_head, bc_own...  131 us
    dot_general x3, matrix products, state_space(): jnp.einsum('bcijh,bcjhp->bcihp', mixing_table, weighted, precision=precise)  47.4 us
    reduce_scatter x1, waiting for transfers between devices, on_device(): lax.psum_scatter(partial_in, 'tensor', scatter_dimension=0, tiled=True)  42.4 us
    psum x1, blocking collectives, on_device(): lax.psum((norm_part, shared_part, wide_conv, wide_gate, wide_head, bc_own...  41.4 us
    all_gather x1, waiting for transfers between devices, on_device(): lax.all_gather(proj_out.astype(jnp.bfloat16), 'dp', axis=0, tiled=True)  38.2 us
    psum x1, blocking collectives, on_device(): d_bc_raw = lax.psum(d_bc_part, 'tensor')  27.6 us
    all_gather x1, blocking collectives, on_device(): lax.all_gather(proj_dt.astype(jnp.bfloat16), 'dp', axis=0, tiled=True)  23.3 us
  transfers between devices with their start and end apart: 10, of which 7 were waited for; matrix products, arithmetic and copies ran while one was open for 17% of the time, Pallas kernels for 0%

commit v1 on v0

v1 whole, which is shorter than its diff:
```python
import functools

import jax
import jax.numpy as jnp
from jax import lax
from jax.experimental import pallas as pl
from jax.experimental.pallas import tpu as pltpu
from jax.sharding import PartitionSpec as P

HEAD_DIM = 64
SPAN = 256
LEN = 512
STEP = 3
INNER = 1536


epsilon = 1e-05
precise = lax.Precision.HIGHEST
beta_first = 0.9
beta_second = 0.95
learn_rate = 0.1
weight_decay = 0.01
adam_epsilon = 1e-08


def conv_silu(values, kernel, seq_count):
    kernel_taps = kernel.shape[0] - 1
    shaped = values.reshape(seq_count, LEN, values.shape[1])
    padded = jnp.pad(shaped, ((0, 0), (kernel_taps - 1, 0), (0, 0)))
    summed = kernel[kernel_taps] + jnp.zeros_like(shaped)
    for offset in range(kernel_taps):
        summed = summed + kernel[offset] * padded[:, offset : offset + LEN]
    return jax.nn.silu(summed).reshape(values.shape)


nn_dims = (((1,), (0,)), ((), ()))
nt_dims = (((1,), (1,)), ((), ()))
tn_dims = (((0,), (0,)), ((), ()))
far_below = -1e30


def halves(value):
    high = value.astype(jnp.bfloat16)
    return high, (value - high.astype(jnp.float32)).astype(jnp.bfloat16)


def dot_split(left, right, dims):
    dot = functools.partial(
        lax.dot_general, dimension_numbers=dims, preferred_element_type=jnp.float32
    )
    return dot(left[0], right[0]) + (dot(left[0], right[1]) + dot(left[1], right[0]))


def pick(pair, rows):
    return pair[0][rows], pair[1][rows]


def head_column(table, lane, head):
    return jnp.sum(jnp.where(lane == head, table, 0.0), axis=1, keepdims=True)


def per_lane(columns, width):
    lane = lax.broadcasted_iota(jnp.int32, (1, width), 1)
    result = columns[0]
    for item in range(1, len(columns)):
        result = jnp.where(lane >= item * HEAD_DIM, columns[item], result)
    return jnp.broadcast_to(result, (columns[0].shape[0], width))


def in_head(width, item):
    lane = lax.broadcasted_iota(jnp.int32, (1, width), 1)
    return (lane >= item * HEAD_DIM) & (lane < (item + 1) * HEAD_DIM)


def forward_kernel(group, u_ref, dt_ref, cum_ref, row_ref, bc_ref, skip_ref, y_ref, scores):
    step = pl.program_id(1)
    width = u_ref.shape[1]
    state_dim = bc_ref.shape[1] // 2

    @pl.when(step == 0)
    def _():
        keys, queries = halves(bc_ref[:, :state_dim]), halves(bc_ref[:, state_dim:])
        scores[...] = dot_split(queries, keys, nt_dims)

    lane = lax.broadcasted_iota(jnp.int32, dt_ref.shape, 1)
    dts = [head_column(dt_ref[...], lane, step * group + item) for item in range(group)]
    cums = [head_column(cum_ref[...], lane, step * group + item) for item in range(group)]
    weighted = halves(u_ref[...] * per_lane(dts, width))
    for block in range(LEN // SPAN):
        rows = slice(block * SPAN, (block + 1) * SPAN)
        past = slice(0, (block + 1) * SPAN)
        shape = (SPAN, (block + 1) * SPAN)
        mask = (
            lax.broadcasted_iota(jnp.int32, shape, 0) + block * SPAN
            >= lax.broadcasted_iota(jnp.int32, shape, 1)
        )
        total = skip_ref[...] * u_ref[rows, :]
        for item in range(group):
            row = row_ref[0, pl.ds(step * group + item, 1), past]
            decay = jnp.exp(jnp.where(mask, cums[item][rows] - row, far_below))
            mixing_table = halves(scores[rows, past] * decay)
            part = dot_split(mixing_table, pick(weighted, past), nn_dims)
            total = total + jnp.where(in_head(width, item), part, 0.0)
        y_ref[rows, :] = total


def backward_kernel(
    group,
    dy_ref,
    y_ref,
    u_ref,
    dt_ref,
    cum_ref,
    row_ref,
    bc_ref,
    skip_ref,
    du_ref,
    ddt_ref,
    dcum_ref,
    dskip_ref,
    dbc_ref,
    scores,
    d_scores,
):
    step = pl.program_id(1)
    width = u_ref.shape[1]
    state_dim = bc_ref.shape[1] // 2

    @pl.when(step == 0)
    def _():
        keys, queries = halves(bc_ref[:, :state_dim]), halves(bc_ref[:, state_dim:])
        scores[...] = dot_split(keys, queries, nt_dims)
        d_scores[...] = jnp.zeros_like(d_scores)
        ddt_ref[...] = jnp.zeros_like(ddt_ref)
        dcum_ref[...] = jnp.zeros_like(dcum_ref)
        dskip_ref[...] = jnp.zeros_like(dskip_ref)

    lane = lax.broadcasted_iota(jnp.int32, dt_ref.shape, 1)
    dts = [head_column(dt_ref[...], lane, step * group + item) for item in range(group)]
    cums = [head_column(cum_ref[...], lane, step * group + item) for item in range(group)]
    dt_lanes = per_lane(dts, width)
    weighted = u_ref[...] * dt_lanes
    split_w = halves(weighted)
    split_dy = halves(dy_ref[...])
    for block in range(LEN // SPAN):
        rows = slice(block * SPAN, (block + 1) * SPAN)
        later = slice(block * SPAN, LEN)
        shape = (SPAN, LEN - block * SPAN)
        mask = lax.broadcasted_iota(jnp.int32, shape, 0) <= lax.broadcasted_iota(
            jnp.int32, shape, 1
        )
        dy_later = pick(split_dy, later)
        dw = jnp.zeros((SPAN, width), jnp.float32)
        d_block = jnp.zeros(shape, jnp.float32)
        for item in range(group):
            inside = in_head(width, item)
            row = row_ref[0, pl.ds(step * group + item, 1), later]
            decay = jnp.exp(jnp.where(mask, row - cums[item][rows], far_below))
            mixing_table = halves(scores[rows, later] * decay)
            part = dot_split(mixing_table, dy_later, nn_dims)
            dw = dw + jnp.where(inside, part, 0.0)
            own = halves(jnp.where(inside, weighted[rows], 0.0))
            d_block = d_block + dot_split(own, dy_later, nt_dims) * decay
        d_scores[rows, later] += d_block
        u = u_ref[rows, :]
        dy = dy_ref[rows, :]
        du_ref[rows, :] = dw * dt_lanes[rows] + skip_ref[...] * dy
        dw_u = dw * u
        dy_u = dy * u
        balance = dy * (y_ref[rows, :] - skip_ref[...] * u) - weighted[rows] * dw
        for item in range(group):
            inside = in_head(width, item)
            here = lane[rows] == step * group + item
            for ref, value in ((ddt_ref, dw_u), (dcum_ref, balance), (dskip_ref, dy_u)):
                column = jnp.sum(jnp.where(inside, value, 0.0), axis=1, keepdims=True)
                ref[rows, :] += jnp.where(here, column, 0.0)

    @pl.when(step == pl.num_programs(1) - 1)
    def _():
        keys, queries = halves(bc_ref[:, :state_dim]), halves(bc_ref[:, state_dim:])
        split_d = halves(d_scores[...])
        dbc_ref[:, :state_dim] = dot_split(split_d, queries, nn_dims)
        dbc_ref[:, state_dim:] = dot_split(split_d, keys, tn_dims)


def mixer_specs(heads, inner):
    group = 2 if heads % 2 == 0 else heads
    width = inner * group // heads
    wide = pl.BlockSpec((LEN, width), lambda seq, step: (seq, step))
    table = pl.BlockSpec((LEN, heads), lambda seq, step: (seq, 0))
    lines = pl.BlockSpec((1, heads, LEN), lambda seq, step: (seq, 0, 0))
    skip = pl.BlockSpec((1, width), lambda seq, step: (0, step))
    return group, wide, table, lines, skip


def mixer_forward(u, step_size, cum, cum_rows, bc_conv, skip_lanes):
    tokens, inner = u.shape
    heads = step_size.shape[1]
    group, wide, table, lines, skip = mixer_specs(heads, inner)
    shared = pl.BlockSpec((LEN, bc_conv.shape[1]), lambda seq, step: (seq, 0))
    return pl.pallas_call(
        functools.partial(forward_kernel, group),
        out_shape=jax.ShapeDtypeStruct(u.shape, jnp.float32),
        grid=(tokens // LEN, heads // group),
        in_specs=[wide, table, table, lines, shared, skip],
        out_specs=wide,
        scratch_shapes=[pltpu.VMEM((LEN, LEN), jnp.float32)],
        name="mixer_forward",
    )(u, step_size, cum, cum_rows, bc_conv, skip_lanes)


def mixer_backward(dy, y, u, step_size, cum, cum_rows, bc_conv, skip_lanes):
    tokens, inner = u.shape
    heads = step_size.shape[1]
    group, wide, table, lines, skip = mixer_specs(heads, inner)
    shared = pl.BlockSpec((LEN, bc_conv.shape[1]), lambda seq, step: (seq, 0))
    small = jax.ShapeDtypeStruct(step_size.shape, jnp.float32)
    return pl.pallas_call(
        functools.partial(backward_kernel, group),
        out_shape=(
            jax.ShapeDtypeStruct(u.shape, jnp.float32),
            small,
            small,
            small,
            jax.ShapeDtypeStruct(bc_conv.shape, jnp.float32),
        ),
        grid=(tokens // LEN, heads // group),
        in_specs=[wide, wide, wide, table, table, lines, shared, skip],
        out_specs=(wide, table, table, table, shared),
        scratch_shapes=[pltpu.VMEM((LEN, LEN), jnp.float32)] * 2,
        name="mixer_backward",
    )(dy, y, u, step_size, cum, cum_rows, bc_conv, skip_lanes)


def shift(value, axis, count, offset):
    return lax.ppermute(value, axis, [(i, (i + offset) % count) for i in range(count)])


def gather_rows(value, axis):
    count, me = lax.axis_size(axis), lax.axis_index(axis)
    rows = value.shape[0]
    whole = jnp.zeros((count * rows,) + value.shape[1:], value.dtype)
    for offset in range(count):
        piece = shift(value, axis, count, offset) if offset else value
        source = lax.rem(me + count - offset, count)
        whole = lax.dynamic_update_slice_in_dim(whole, piece, source * rows, 0)
    return whole


def scatter_rows(value, axis, kind):
    count, me = lax.axis_size(axis), lax.axis_index(axis)
    rows = value.shape[0] // count
    total = lax.dynamic_slice_in_dim(value, me * rows, rows, 0)
    for offset in range(1, count):
        target = lax.rem(me + offset, count)
        piece = lax.dynamic_slice_in_dim(value, target * rows, rows, 0).astype(kind)
        total = total + shift(piece, axis, count, offset).astype(jnp.float32)
    return total


def butterfly_ok(axis):
    count = lax.axis_size(axis)
    return count & (count - 1) == 0


def flip(value, axis, bit):
    count = lax.axis_size(axis)
    return lax.ppermute(value, axis, [(i, i ^ bit) for i in range(count)])


def sum_all(value, axis):
    if not butterfly_ok(axis):
        return lax.psum(value, axis)
    bit = 1
    while bit < lax.axis_size(axis):
        value = value + flip(value, axis, bit)
        bit *= 2
    return value


def scatter_halving(value, axis):
    if not butterfly_ok(axis):
        return lax.psum_scatter(value, axis, scatter_dimension=0, tiled=True)
    count, me = lax.axis_size(axis), lax.axis_index(axis)
    rows = value.shape[0] // count
    tail = value.shape[1:]
    bit = 1
    while bit < count:
        count_left = count // (2 * bit)
        value = value.reshape((count_left, 2, rows) + tail)
        mine = lax.rem(me // bit, 2)
        keep = lax.dynamic_index_in_dim(value, mine, 1, keepdims=False)
        give = lax.dynamic_index_in_dim(value, 1 - mine, 1, keepdims=False)
        moved = flip(give, axis, bit)
        value = keep + moved
        bit *= 2
    return value.reshape((rows,) + tail)


def adam_update(weight, moment, second, gradient):
    moment_new = beta_first * moment + (1.0 - beta_first) * gradient
    second_new = beta_second * second + (1.0 - beta_second) * gradient * gradient
    corr_first = 1.0 - beta_first**STEP
    corr_second = 1.0 - beta_second**STEP
    update = moment_new / corr_first / (jnp.sqrt(second_new / corr_second) + adam_epsilon)
    return (weight - learn_rate * (update + weight_decay * weight), moment_new, second_new)


def whole_step(
    hidden_in,
    cotangent,
    proj_zx,
    proj_dt,
    proj_bc,
    proj_out,
    norm_gain,
    conv_inner,
    conv_shared,
    head_table,
    gate_gain,
    mom_zx,
    mom_dt,
    mom_bc,
    mom_out,
    mom_norm,
    mom_conv,
    mom_shared,
    mom_head,
    mom_gate,
    var_zx,
    var_dt,
    var_bc,
    var_out,
    var_norm,
    var_conv,
    var_shared,
    var_head,
    var_gate,
):
    inner_local = proj_out.shape[1]
    heads_local = proj_dt.shape[1]
    shard_rows = proj_zx.shape[0]
    columns = (2 * inner_local, proj_bc.shape[1], heads_local)
    cot_all = gather_rows(cotangent.astype(jnp.bfloat16), "tensor")
    scale_in = lax.rsqrt(jnp.mean(hidden_in * hidden_in, axis=-1, keepdims=True) + epsilon)
    unit_in = hidden_in * scale_in
    normed_local = (unit_in * norm_gain).astype(jnp.bfloat16)
    normed = gather_rows(normed_local, "tensor")
    packed = jnp.concatenate(
        [proj_zx.reshape(shard_rows, columns[0]), proj_out, proj_bc, proj_dt], axis=1
    ).astype(jnp.bfloat16)
    full_in = lax.all_gather(packed, "dp", axis=0, tiled=True)
    full_z = full_in[:, :inner_local]
    full_x = full_in[:, inner_local : columns[0]]
    bc_start = columns[0] + inner_local
    full_out = full_in[:, columns[0] : bc_start]
    full_bc = full_in[:, bc_start : bc_start + columns[1]]
    full_dt = full_in[:, bc_start + columns[1] :]
    seq_count = normed.shape[0] // LEN
    x_raw = jnp.dot(normed, full_x, preferred_element_type=jnp.float32)
    bc_raw = jnp.dot(normed, full_bc, preferred_element_type=jnp.float32)
    dt_raw = jnp.dot(normed, full_dt, preferred_element_type=jnp.float32)
    gate_pre = jnp.dot(normed, full_z, preferred_element_type=jnp.float32)
    x_conv, pull_inner = jax.vjp(lambda v, k: conv_silu(v, k, seq_count), x_raw, conv_inner)
    bc_conv, pull_shared = jax.vjp(lambda v, k: conv_silu(v, k, seq_count), bc_raw, conv_shared)
    dt_pre = dt_raw + head_table[0]
    step_size = jax.nn.softplus(dt_pre)
    decay_rate = -jnp.exp(head_table[1])
    position = jnp.arange(LEN)
    lower = (position[:, None] >= position[None, :]).astype(jnp.float32)
    rates = (step_size * decay_rate).reshape(seq_count, LEN, heads_local)
    cum = jnp.einsum("ts,bsh->bth", lower, rates, precision=precise)
    cum_rows = jnp.swapaxes(cum, 1, 2)
    cum = cum.reshape(step_size.shape)
    skip_lanes = jnp.repeat(head_table[2], HEAD_DIM)[None]
    mixer_out = mixer_forward(x_conv, step_size, cum, cum_rows, bc_conv, skip_lanes)
    gate_act = jax.nn.silu(gate_pre)
    gated_out = mixer_out * gate_act
    d_gate_out = jnp.dot(cot_all, full_out, preferred_element_type=jnp.float32)
    d_unit = d_gate_out * gate_gain
    square_sum, gated_dot = sum_all(
        jnp.stack(
            [jnp.sum(gated_out * gated_out, axis=-1), jnp.sum(d_unit * gated_out, axis=-1)]
        ),
        "tensor",
    )
    scale_gate = lax.rsqrt(square_sum / INNER + epsilon)[:, None]
    unit_gate = gated_out * scale_gate
    normed_gate = (unit_gate * gate_gain).astype(jnp.bfloat16)
    inner_dot = gated_dot * scale_gate[:, 0]
    grad_out_group = jnp.dot(cot_all.T, normed_gate, preferred_element_type=jnp.float32)
    grad_out = scatter_halving(grad_out_group, "dp")
    branch_full = jnp.dot(normed_gate, full_out.T, preferred_element_type=jnp.float32)
    branch_out = scatter_rows(branch_full, "tensor", jnp.bfloat16)
    hidden_out = hidden_in + branch_out
    gate_part = jnp.sum(d_gate_out * unit_gate, axis=0)
    d_gated = scale_gate * (d_unit - unit_gate * (inner_dot / INNER)[:, None])
    d_mixer = d_gated * gate_act
    sigm = jax.nn.sigmoid(gate_pre)
    d_z16 = (d_gated * mixer_out * sigm * (1.0 + gate_pre * (1.0 - sigm))).astype(jnp.bfloat16)
    z_group = jnp.dot(normed.T, d_z16, preferred_element_type=jnp.float32)
    grad_z = scatter_halving(z_group, "dp")
    d_conv, d_step, d_cum, d_skip, d_bc_conv = mixer_backward(
        d_mixer, mixer_out, x_conv, step_size, cum, cum_rows, bc_conv, skip_lanes
    )
    d_bc_part, shared_part = pull_shared(d_bc_conv)
    own_bc = scatter_rows(d_bc_part, "tensor", jnp.float32).astype(jnp.bfloat16)
    d_x_raw, conv_part = pull_inner(d_conv)
    d_rates = jnp.einsum(
        "ts,bth->bsh", lower, d_cum.reshape(rates.shape), precision=precise
    ).reshape(step_size.shape)
    d_dt_raw = (d_step + d_rates * decay_rate) * jax.nn.sigmoid(dt_pre)
    head_part = jnp.stack(
        [
            jnp.sum(d_dt_raw, axis=0),
            jnp.sum(d_rates * step_size, axis=0) * decay_rate,
            jnp.sum(d_skip, axis=0),
        ]
    )
    d_x16 = d_x_raw.astype(jnp.bfloat16)
    d_dt16 = d_dt_raw.astype(jnp.bfloat16)
    x_group = jnp.dot(normed.T, d_x16, preferred_element_type=jnp.float32)
    grad_x = scatter_halving(x_group, "dp")
    dt_group = jnp.dot(normed.T, d_dt16, preferred_element_type=jnp.float32)
    bc_own = jnp.dot(normed_local.T, own_bc, preferred_element_type=jnp.float32)
    partial_in = jnp.dot(d_z16, full_z.T, preferred_element_type=jnp.float32)
    partial_in = partial_in + jnp.dot(d_x16, full_x.T, preferred_element_type=jnp.float32)
    partial_in = partial_in + jnp.dot(d_dt16, full_dt.T, preferred_element_type=jnp.float32)
    d_normed = scatter_rows(partial_in, "tensor", jnp.bfloat16)
    d_normed = d_normed + jnp.dot(own_bc, full_bc.T, preferred_element_type=jnp.float32)
    norm_part = jnp.sum(d_normed * unit_in, axis=0)
    d_unit_in = d_normed * norm_gain
    grad_hidden = cotangent + scale_in * (
        d_unit_in - unit_in * jnp.mean(d_unit_in * unit_in, axis=-1, keepdims=True)
    )
    side = scatter_halving(jnp.concatenate([bc_own, dt_group], axis=1), "dp")
    grad_bc = sum_all(side[:, : columns[1]], "tensor")
    grad_dt = side[:, columns[1] :]
    grad_zx = jnp.stack([grad_z, grad_x], axis=1)
    parts = (conv_part, gate_part, head_part, shared_part, norm_part)
    flat = sum_all(jnp.concatenate([part.reshape(-1) for part in parts]), "dp")
    sums = []
    offset = 0
    for part in parts:
        sums.append(flat[offset : offset + part.size].reshape(part.shape))
        offset += part.size
    grad_conv, grad_gate, grad_head = sums[:3]
    both = sum_all(jnp.concatenate([sums[3].reshape(-1), sums[4]]), "tensor")
    sum_shared = both[: shared_part.size].reshape(shared_part.shape)
    sum_norm = both[shared_part.size :]
    grads = (
        grad_zx,
        grad_dt,
        grad_bc,
        grad_out,
        sum_norm,
        grad_conv,
        sum_shared,
        grad_head,
        grad_gate,
    )
    weights = (
        proj_zx,
        proj_dt,
        proj_bc,
        proj_out,
        norm_gain,
        conv_inner,
        conv_shared,
        head_table,
        gate_gain,
    )
    moments = (mom_zx, mom_dt, mom_bc, mom_out, mom_norm, mom_conv, mom_shared, mom_head, mom_gate)
    seconds = (var_zx, var_dt, var_bc, var_out, var_norm, var_conv, var_shared, var_head, var_gate)
    results = [
        adam_update(w_item, m_item, v_item, g_item)
        for w_item, m_item, v_item, g_item in zip(weights, moments, seconds, grads)
    ]
    new_weights = tuple((item[0] for item in results))
    new_moments = tuple((item[1] for item in results))
    new_seconds = tuple((item[2] for item in results))
    return (hidden_out, grad_hidden) + grads + new_weights + new_moments + new_seconds


def solution(mesh):
    placed = (
        P(("dp", "tensor"), None),
        P(("dp", "tensor"), None),
        P("dp", None, "tensor"),
        P("dp", "tensor"),
        P("dp", None),
        P("dp", "tensor"),
        P(),
        P(None, "tensor"),
        P(),
        P(None, "tensor"),
        P("tensor"),
        P("dp", None, "tensor"),
        P("dp", "tensor"),
        P("dp", None),
        P("dp", "tensor"),
        P(),
        P(None, "tensor"),
        P(),
        P(None, "tensor"),
        P("tensor"),
        P("dp", None, "tensor"),
        P("dp", "tensor"),
        P("dp", None),
        P("dp", "tensor"),
        P(),
        P(None, "tensor"),
        P(),
        P(None, "tensor"),
        P("tensor"),
    )
    return jax.shard_map(
        whole_step,
        mesh=mesh,
        in_specs=placed,
        out_specs=(
            P(("dp", "tensor"), None),
            P(("dp", "tensor"), None),
            P("dp", None, "tensor"),
            P("dp", "tensor"),
            P("dp", None),
            P("dp", "tensor"),
            P(),
            P(None, "tensor"),
            P(),
            P(None, "tensor"),
            P("tensor"),
            P("dp", None, "tensor"),
            P("dp", "tensor"),
            P("dp", None),
            P("dp", "tensor"),
            P(),
            P(None, "tensor"),
            P(),
            P(None, "tensor"),
            P("tensor"),
            P("dp", None, "tensor"),
            P("dp", "tensor"),
            P("dp", None),
            P("dp", "tensor"),
            P(),
            P(None, "tensor"),
            P(),
            P(None, "tensor"),
            P("tensor"),
            P("dp", None, "tensor"),
            P("dp", "tensor"),
            P("dp", None),
            P("dp", "tensor"),
            P(),
            P(None, "tensor"),
            P(),
            P(None, "tensor"),
            P("tensor"),
        ),
        check_vma=False,
    )
```

time: 898 us -> 329 us (0.37)
  waiting for transfers between devices: 413 us -> 94.9 us
  blocking collectives: 123 us -> 0 us
  matrix products: 129 us -> 39 us
  local copies, waits for them, and re-layouts: 93.6 us -> 30.6 us
  Pallas kernels: 0 us -> 45.9 us
  other arithmetic: 110 us -> 68 us
  starting transfers between devices: 0.42 us -> 28.8 us
    unnamed x13 -> x1, waiting for transfers between devices: 187 us -> 0.02 us
    psum x1 -> x0, waiting for transfers between devices: 131 us -> none  [on_device(): lax.psum((norm_part, shared_part, wide_conv, wide_gate, wide_head, bc_own...]
    dot_general x23 -> x17, matrix products: 128 us -> 39 us  [the longest x1 6.37 us: whole_step(): d_gate_out = jnp.dot(cot_all, full_out, preferred_element_type=jnp.float32)]
    ppermute x0 -> x28, waiting for transfers between devices: none -> 83.3 us  [the longest x23 50 us: flip(): return lax.ppermute(value, axis, [(i, i ^ bit) for i in range(count)])]
    psum x4 -> x0, blocking collectives: 79.5 us -> none  [the longest x1 41.4 us: on_device(): lax.psum((norm_part, shared_part, wide_conv, wide_gate, wide_head, bc_own...]
    pallas_call x0 -> x2, Pallas kernels: none -> 45.9 us  [the longest x1 29.7 us: mixer_backward(): pl.pallas_call(functools.partial(backward_kernel, group), out_shape=(jax....]
    reshape x14 -> x5, local copies, waits for them, and re-layouts: 44.2 us -> 0.17 us  [the longest x3 0.09 us: whole_step(): flat = sum_all(jnp.concatenate([part.reshape(-1) for part in parts]), 'dp')]
    all_gather x2 -> x0, blocking collectives: 43.3 us -> none  [the longest x1 23.3 us: on_device(): lax.all_gather(proj_dt.astype(jnp.bfloat16), 'dp', axis=0, tiled=True)]
  transfers between devices with their start and end apart: 10 -> 29, of which waited for: 7 -> 16; matrix products, arithmetic and copies ran while one was open for 17% -> 27% of each run, Pallas kernels for 0% -> 0%
where the time goes in v1:
time: 329 us; the launch traced here: 323 us
  waiting for transfers between devices  94.9 us (29%)
  other arithmetic  68 us (21%)
  Pallas kernels  45.9 us (14%)
  matrix products  39 us (12%)
  local copies, waits for them, and re-layouts  30.6 us (9%)
  starting transfers between devices  28.8 us (9%)
  between operations  15.4 us (5%)
    ppermute x23, waiting for transfers between devices, flip(): return lax.ppermute(value, axis, [(i, i ^ bit) for i in range(count)])  50 us
    ppermute x5, waiting for transfers between devices, shift(): lax.ppermute(value, axis, [(i, (i + offset) % count) for i in range(count)])  33.4 us
    pallas_call x1, Pallas kernels, mixer_backward(): pl.pallas_call(functools.partial(backward_kernel, group), out_shape=(jax....  29.7 us
    ppermute x23, starting transfers between devices, flip(): return lax.ppermute(value, axis, [(i, i ^ bit) for i in range(count)])  22.2 us
    pallas_call x1, Pallas kernels, mixer_forward(): pl.pallas_call(functools.partial(forward_kernel, group), out_shape=jax.Sh...  16.2 us
    reduce_sum x2, other arithmetic, conv_silu(): summed = summed + kernel[offset] * padded[:, offset:offset + LEN]  15.6 us
    all_gather x1, waiting for transfers between devices, whole_step(): full_in = lax.all_gather(packed, 'dp', axis=0, tiled=True)  11.6 us
    add x12, other arithmetic, scatter_halving(): value = keep + moved  9.66 us
  transfers between devices with their start and end apart: 29, of which 16 were waited for; matrix products, arithmetic and copies ran while one was open for 27% of the time, Pallas kernels for 0%

profile of v1, /device:TPU:0, one launch (start us, length us, event | category | flops | bytes accessed | tf_op | source)
XLA Modules:
  0.0 322.8 jit_solution(1453772127501401258)
XLA Ops:
  13.6 3.0 collective-permute-start
  16.7 2.4 constant_dynamic-update-slice_fusion.1
  20.7 14.4 %collective-permute-done = bf16[512,768]{1,0:T(8,128)(2,1)} collective-permute-done((bf16[512,768]{1,0:T(8,128)(2,1)S(1)}, bf16[512,768]{1,0:T(8,128)(2,1)}, u32[]{:S(2)}, u32[]{:S(2)}) %collective-permute-start) | collective-permute-done | bytes 786464 | tf_op jit(solution)/shard_map/ppermute | solution.py:236
  36.7 14.5 %collective-permute-done.1 = bf16[512,768]{1,0:T(8,128)(2,1)} collective-permute-done((bf16[512,768]{1,0:T(8,128)(2,1)}, bf16[512,768]{1,0:T(8,128)(2,1)}, u32[]{:S(2)}, u32[]{:S(2)}) %collective-permute-start.1) | collective-permute-done | bytes 786464 | tf_op jit(solution)/shard_map/ppermute | solution.py:236
  53.2 11.6 %all-gather.2.cloned.1.call-done = bf16[768,2572]{1,0:T(8,128)(2,1)} async-done(((bf16[48,2572]{1,0:T(8,128)(2,1)}), bf16[768,2572]{1,0:T(8,128)(2,1)}) %all-gather.2.cloned.1.call-update) | async-done | bytes 3950608 | tf_op jit(solution)/shard_map/all_gather | solution.py:352
  64.8 2.6 broadcast_multiply_fusion.8
  73.9 2.7 fusion.23
  76.7 4.1 %fusion.4 = (f32[2,512,768]{2,1,0:T(8,128)}, f32[2,512,768]{2,1,0:T(8,128)}) fusion(f32[2,512,768]{2,1,0:T(8,128)S(1)} %bitcast.154, f32[768]{0:T(1024)S(1)} %get-tuple-element.186, f32[768]{0:T(1024)S(1)} %get-tuple-element.183, f32[768]{0:T(1024)S(1)} %get-tuple-element.184, f32[768]{0:T(1024)S(1)} %get-tuple-element.185, f32[768]{0:T(1024)S(1)} %get-tuple-element.182), kind=kLoop, calls=%fused_computation.21 | loop fusion | flops 9437184 | bytes 9452544 | tf_op jit(solution)/shard_map/jvp(jit(silu))/mul | solution.py:33
  80.8 16.2 %mixer_forward.1.y_ref = f32[1024,768]{1,0:T(8,128)} custom-call(f32[1024,768]{1,0:T(8,128)} %bitcast.156, f32[1024,12]{1,0:T(8,128)} %get-tuple-element.244.dt_ref, f32[1024,12]{1,0:T(8,128)} %bitcast.163, f32[2,12,512]{2,1,0:T(8,128)} %copy-done.33, f32[1024,256]{1,0:T(8,128)} %bitcast.161, f32[1,768]{1,0:T(1,128)} %broadcast_in_dim_reshape.3.skip_ref), custom_call_target="tpu_custom_call" | custom-call | tf_op jit(solution)/shard_map/mixer_forward/pallas_call | solution.py:201
  97.0 3.3 %fusion.19 = f32[1024,768]{1,0:T(8,128)S(1)} fusion(bf16[1024,768]{0,1:T(8,128)(2,1)} %copy-done.4, bf16[768,2572]{1,0:T(8,128)(2,1)} %all-gather.2.cloned.1.call-done), kind=kOutput, calls=%fused_computation.70 | convolution fusion | flops 1207959552 | bytes 5898240 | tf_op jit(solution)/shard_map/dot_general | solution.py:363
  100.4 6.4 %multiply_reduce_fusion.6 = (f32[1024]{0:T(1024)S(1)}, f32[1024]{0:T(1024)S(1)}, f32[1024,768]{1,0:T(8,128)}, f32[1024,768]{1,0:T(8,128)}) fusion(f32[768]{0:T(1024)S(1)} %copy-done.49, f32[1024,768]{1,0:T(8,128)S(1)} %copy-done, f32[1024,768]{1,0:T(8,128)S(1)} %fusion.19, bf16[1024,768]{1,0:T(8,128)(2,1)S(1)} %copy-done.31, ...), kind=kOutput, calls=%fused_computation.17 | convolution fusion | flops 1215821824 | bytes 15346688 | tf_op jit(solution)/shard_map/dot_general | solution.py:379
  110.6 5.5 %fusion.54 = f32[768,768]{1,0:T(8,128)} fusion(bf16[1024,768]{1,0:T(8,128)(2,1)} %constant_dynamic-update-slice_fusion, f32[1024,768]{1,0:T(8,128)} %get-tuple-element.222, f32[1024]{0:T(1024)S(1)} %bitcast.197, f32[768]{0:T(1024)S(1)} %copy-done.49), kind=kOutput, calls=%fused_computation.194 | convolution fusion | flops 1210318848 | bytes 7085056 | tf_op jit(solution)/shard_map/dot_general | solution.py:391
  116.1 5.2 %fusion.5 = (f32[1024,768]{1,0:T(8,128)}, bf16[1024,768]{1,0:T(8,128)(2,1)}, f32[768]{0:T(1024)S(1)}) fusion(f32[1024]{0:T(1024)S(1)} %multiply_multiply_fusion.8, f32[1024,768]{1,0:T(8,128)S(1)} %copy-done.7, f32[1024,768]{1,0:T(8,128)} %get-tuple-element.257, f32[1024]{0:T(1024)S(1)} %bitcast.198, f32[768]{0:T(1024)S(1)} %copy-done.49, ...), kind=kLoop, calls=%fused_computation.31 | loop fusion | flops 14941440 | bytes 17315840 | tf_op jit(solution)/shard_map/mul | solution.py:398
  121.3 29.7 %mixer_backward.1 = (f32[1024,768]{1,0:T(8,128)}, f32[1024,12]{1,0:T(8,128)}, f32[1024,12]{1,0:T(8,128)}, f32[1024,12]{1,0:T(8,128)}, f32[1024,256]{1,0:T(8,128)}) custom-call(f32[1024,768]{1,0:T(8,128)} %get-tuple-element.229.dy_ref, f32[1024,768]{1,0:T(8,128)} %mixer_forward.1.y_ref, f32[1024,768]{1,0:T(8,128)} %bitcast.157, ...), custom_call_target="tpu_custom_call" | custom-call | tf_op jit(solution)/shard_map/mixer_backward/pallas_call | solution.py:218
  151.0 4.2 %multiply_reduce_fusion.13 = (f32[256]{0:T(256)S(1)}, f32[256]{0:T(256)S(1)}, f32[256]{0:T(256)S(1)}, f32[256]{0:T(256)S(1)}, f32[256]{0:T(256)S(1)}, /*index=5*/f32[2,512,256]{2,1,0:T(8,128)S(1)}) fusion(f32[1024,256]{1,0:T(8,128)} %copy-done.16, f32[2,512,256]{2,1,0:T(8,128)} %bitcast.160, f32[2,512,256]{2,1,0:T(8,128)} %get-tuple-element.226, ...), kind=kLoop, calls=%fused_computation.57 | loop fusion | flops 4717312 | bytes 5248000 | tf_op jit(solution)/shard_map/transpose(jvp())/reduce_sum | solution.py:32
  158.9 11.4 %multiply_reduce_fusion.4 = (f32[768]{0:T(1024)S(1)}, f32[768]{0:T(1024)S(1)}, f32[768]{0:T(1024)S(1)}, f32[768]{0:T(1024)S(1)}, f32[768]{0:T(1024)S(1)}, /*index=5*/f32[2,512,768]{2,1,0:T(8,128)S(1)}) fusion(f32[1024,768]{1,0:T(8,128)S(1)} %fusion.23, f32[2,512,768]{2,1,0:T(8,128)S(1)} %bitcast.155, f32[2,512,768]{2,1,0:T(8,128)S(1)} %copy-done.9, ...), kind=kLoop, calls=%fused_computation.11 | loop fusion | flops 14151936 | bytes 15744000 | tf_op jit(solution)/shard_map/transpose(jvp())/reduce_sum | solution.py:32
  170.4 4.7 %broadcast_multiply_fusion = (f32[2,512,768]{2,1,0:T(8,128)}, f32[2,512,768]{2,1,0:T(8,128)}, f32[2,512,768]{2,1,0:T(8,128)}, f32[2,512,768]{2,1,0:T(8,128)}) fusion(f32[2,512,768]{2,1,0:T(8,128)S(1)} %get-tuple-element.221, f32[768]{0:T(1024)S(1)} %get-tuple-element.186, f32[768]{0:T(1024)S(1)} %get-tuple-element.185, f32[768]{0:T(1024)S(1)} %get-tuple-element.184, ...), kind=kLoop, calls=%fused_computation.34 | loop fusion | flops 3145728 | bytes 15740928 | tf_op jit(solution)/shard_map/transpose(jvp())/mul | solution.py:32
  175.9 2.9 fusion.72
  180.7 3.0 fusion.2
  198.9 2.5 dynamic-slice_bitcast_fusion
  203.6 2.4 fusion.74
  206.1 4.5 %collective-permute-done.4 = bf16[512,768]{1,0:T(8,128)(2,1)} collective-permute-done((bf16[512,768]{1,0:T(8,128)(2,1)}, bf16[512,768]{1,0:T(8,128)(2,1)}, u32[]{:S(2)}, u32[]{:S(2)}) %collective-permute-start.4) | collective-permute-done | bytes 786464 | tf_op jit(solution)/shard_map/ppermute | solution.py:236
  210.6 3.1 multiply_reduce_fusion.7
  216.0 2.6 copy.130
  224.1 2.3 collective-permute-done.25
  228.5 4.5 %multiply_add_fusion.1 = (f32[512,768]{1,0:T(8,128)}, f32[512,768]{1,0:T(8,128)}) fusion(f32[512,768]{1,0:T(8,128)S(1)} %copy-done.18, f32[512,768]{1,0:T(8,128)} %get-tuple-element.258, f32[512,768]{1,0:T(8,128)S(1)} %copy-done.3, f32[512]{0:T(512)S(1)} %broadcast_multiply_fusion.9, f32[768]{0:T(1024)S(1)} %copy-done.45, f32[512]{0:T(512)S(1)} %add_rsqrt_fusion, ...), kind=kLoop, calls=%fused_computation.26 | loop fusion | flops 3538944 | bytes 10230788 | tf_op jit(solution)/shard_map/add | solution.py:433
  240.1 7.5 %collective-permute-done.15 = f32[4,48,268]{2,1,0:T(8,128)S(1)} collective-permute-done((f32[4,48,268]{2,1,0:T(8,128)S(1)}, f32[4,48,268]{2,1,0:T(8,128)S(1)}, u32[]{:S(2)}, u32[]{:S(2)}) %collective-permute-start.15) | collective-permute-done | bytes 205856 | tf_op jit(solution)/shard_map/ppermute | solution.py:268
  263.9 2.7 collective-permute-done.18
  270.2 10.0 %collective-permute-done.7 = f32[4,48,768]{2,1,0:T(8,128)} collective-permute-done((f32[4,48,768]{2,1,0:T(8,128)}, f32[4,48,768]{2,1,0:T(8,128)}, u32[]{:S(2)}, u32[]{:S(2)}) %collective-permute-start.7) | collective-permute-done | bytes 589856 | tf_op jit(solution)/shard_map/ppermute | solution.py:268
  283.0 7.4 %collective-permute-done.20 = f32[4,48,768]{2,1,0:T(8,128)} collective-permute-done((f32[4,48,768]{2,1,0:T(8,128)}, f32[4,48,768]{2,1,0:T(8,128)}, u32[]{:S(2)}, u32[]{:S(2)}) %collective-permute-start.20) | collective-permute-done | bytes 589856 | tf_op jit(solution)/shard_map/ppermute | solution.py:268
  296.3 7.6 %collective-permute-done.21 = f32[2,48,768]{2,1,0:T(8,128)S(1)} collective-permute-done((f32[2,48,768]{2,1,0:T(8,128)S(1)}, f32[2,48,768]{2,1,0:T(8,128)S(1)}, u32[]{:S(2)}, u32[]{:S(2)}) %collective-permute-start.21) | collective-permute-done | bytes 294944 | tf_op jit(solution)/shard_map/ppermute | solution.py:268
  304.1 6.7 %collective-permute-done.9 = f32[1,48,768]{2,1,0:T(8,128)S(1)} collective-permute-done((f32[1,48,768]{2,1,0:T(8,128)S(1)}, f32[1,48,768]{2,1,0:T(8,128)S(1)}, u32[]{:S(2)}, u32[]{:S(2)}) %collective-permute-start.9) | collective-permute-done | bytes 147488 | tf_op jit(solution)/shard_map/ppermute | solution.py:268
  (301 shorter events, 95.6 us)
Async XLA Ops:
  7.2 57.5 %all-gather.2.cloned.1.call-start = ((), (), s32[]{:S(2)}) async-start(), calls=%async_computation | async-start | bytes 4386816 | tf_op jit(solution)/shard_map/all_gather | solution.py:352
  13.6 21.5 %collective-permute-start = (bf16[512,768]{1,0:T(8,128)(2,1)S(1)}, bf16[512,768]{1,0:T(8,128)(2,1)}, u32[]{:S(2)}, u32[]{:S(2)}) collective-permute-start(bf16[512,768]{1,0:T(8,128)(2,1)S(1)} %multiply_convert_fusion.2), channel_id=1, source_target_pairs={{0,1},{1,0},{2,3},{3,2},{4,5},{5,4},{6,7},{7,6},{8,9},{9,8},{10,11... | collective-permute-start | bytes 2359304 | tf_op jit(solution)/shard_map/ppermute | solution.py:236
  19.2 32.0 %collective-permute-start.1 = (bf16[512,768]{1,0:T(8,128)(2,1)}, bf16[512,768]{1,0:T(8,128)(2,1)}, u32[]{:S(2)}, u32[]{:S(2)}) collective-permute-start(bf16[512,768]{1,0:T(8,128)(2,1)} %get-tuple-element.224), channel_id=1, source_target_pairs={{0,1},{1,0},{2,3},{3,2},{4,5},{5,4},{6,7},{7,6},{8,9},{9,8},{10,11... | collective-permute-start | bytes 2359304 | tf_op jit(solution)/shard_map/ppermute | solution.py:236
  36.7 34.4 %copy-start.4 = (bf16[1024,768]{0,1:T(8,128)(2,1)}, bf16[1024,768]{0,1:T(8,128)(2,1)S(1)}, u32[]{:S(2)}) copy-start(bf16[1024,768]{0,1:T(8,128)(2,1)S(1)} %constant_dynamic-update-slice_fusion.2) | copy-start | bytes 4718596
  106.8 3.7 %collective-permute-start.2 = (f32[2,1024]{1,0:T(2,128)S(1)}, f32[2,1024]{1,0:T(2,128)S(1)}, u32[]{:S(2)}, u32[]{:S(2)}) collective-permute-start(f32[2,1024]{1,0:T(2,128)S(1)} %pad_maximum_fusion.3), channel_id=1, source_target_pairs={{0,1},{1,0},{2,3},{3,2},{4,5},{5,4},{6,7},{7,6},{8,9},{9,8},{10,11... | collective-permute-start | bytes 24584 | tf_op jit(solution)/shard_map/ppermute | solution.py:268
  156.7 45.3 %collective-permute-start.5 = (f32[512,256]{1,0:T(8,128)}, f32[512,256]{1,0:T(8,128)}, u32[]{:S(2)}, u32[]{:S(2)}) collective-permute-start(f32[512,256]{1,0:T(8,128)} %constant_dynamic-slice_fusion.4), channel_id=1, source_target_pairs={{0,1},{1,0},{2,3},{3,2},{4,5},{5,4},{6,7},{7,6},{8,9},{9,8},{10,11... | collective-permute-start | bytes 1572872 | tf_op jit(solution)/shard_map/ppermute | solution.py:236
  189.8 20.7 %collective-permute-start.4 = (bf16[512,768]{1,0:T(8,128)(2,1)}, bf16[512,768]{1,0:T(8,128)(2,1)}, u32[]{:S(2)}, u32[]{:S(2)}) collective-permute-start(bf16[512,768]{1,0:T(8,128)(2,1)} %dynamic-slice_convert_fusion), channel_id=1, source_target_pairs={{0,1},{1,0},{2,3},{3,2},{4,5},{5,4},{6,7},{7,6},{8,9},{9,8},{10,11... | collective-permute-start | bytes 2359304 | tf_op jit(solution)/shard_map/ppermute | solution.py:236
  193.8 32.6 %collective-permute-start.3 = (bf16[512,768]{1,0:T(8,128)(2,1)}, bf16[512,768]{1,0:T(8,128)(2,1)}, u32[]{:S(2)}, u32[]{:S(2)}) collective-permute-start(bf16[512,768]{1,0:T(8,128)(2,1)} %dynamic-slice_convert_fusion.1), channel_id=1, source_target_pairs={{0,1},{1,0},{2,3},{3,2},{4,5},{5,4},{6,7},{7,6},{8,9},{9,8},{10,11... | collective-permute-start | bytes 2359304 | tf_op jit(solution)/shard_map/ppermute | solution.py:236
  196.9 51.3 %collective-permute-start.10 = (f32[8,48,768]{2,1,0:T(8,128)}, f32[8,48,768]{2,1,0:T(8,128)}, u32[]{:S(2)}, u32[]{:S(2)}) collective-permute-start(f32[8,48,768]{2,1,0:T(8,128)} %dynamic-slice_bitcast_fusion.1), channel_id=1, source_target_pairs={{0,2},{2,0},{4,6},{6,4},{8,10},{10,8},{12,14},{14,12},{16,18},{18,... | collective-permute-start | bytes 3538952 | tf_op jit(solution)/shard_map/ppermute | solution.py:268
  198.1 53.4 %collective-permute-start.6 = (f32[8,48,768]{2,1,0:T(8,128)}, f32[8,48,768]{2,1,0:T(8,128)}, u32[]{:S(2)}, u32[]{:S(2)}) collective-permute-start(f32[8,48,768]{2,1,0:T(8,128)} %dynamic-slice_bitcast_fusion.2), channel_id=1, source_target_pairs={{0,2},{2,0},{4,6},{6,4},{8,10},{10,8},{12,14},{14,12},{16,18},{18,... | collective-permute-start | bytes 3538952 | tf_op jit(solution)/shard_map/ppermute | solution.py:268
  202.0 53.5 %collective-permute-start.19 = (f32[8,48,768]{2,1,0:T(8,128)}, f32[8,48,768]{2,1,0:T(8,128)}, u32[]{:S(2)}, u32[]{:S(2)}) collective-permute-start(f32[8,48,768]{2,1,0:T(8,128)} %dynamic-slice_bitcast_fusion), channel_id=1, source_target_pairs={{0,2},{2,0},{4,6},{6,4},{8,10},{10,8},{12,14},{14,12},{16,18},{18,... | collective-permute-start | bytes 3538952 | tf_op jit(solution)/shard_map/ppermute | solution.py:268
  213.8 4.8 %collective-permute-start.23 = (f32[6692]{0:T(1024)S(1)}, f32[6692]{0:T(1024)S(1)}, u32[]{:S(2)}, u32[]{:S(2)}) collective-permute-start(f32[6692]{0:T(1024)S(1)} %concatenate.15), channel_id=1, source_target_pairs={{0,2},{2,0},{4,6},{6,4},{8,10},{10,8},{12,14},{14,12},{16,18},{18,... | collective-permute-start | bytes 80312 | tf_op jit(solution)/shard_map/ppermute | solution.py:268
  218.6 3.9 %collective-permute-start.24 = (f32[6692]{0:T(1024)S(1)}, f32[6692]{0:T(1024)S(1)}, u32[]{:S(2)}, u32[]{:S(2)}) collective-permute-start(f32[6692]{0:T(1024)S(1)} %add.517), channel_id=1, source_target_pairs={{0,4},{2,6},{4,0},{6,2},{8,12},{10,14},{12,8},{14,10},{16,20},{18,... | collective-permute-start | bytes 80312 | tf_op jit(solution)/shard_map/ppermute | solution.py:268
  222.6 3.9 %collective-permute-start.25 = (f32[6692]{0:T(1024)S(1)}, f32[6692]{0:T(1024)S(1)}, u32[]{:S(2)}, u32[]{:S(2)}) collective-permute-start(f32[6692]{0:T(1024)S(1)} %add.518), channel_id=1, source_target_pairs={{0,8},{2,10},{4,12},{6,14},{8,0},{10,2},{12,4},{14,6},{16,24},{18,... | collective-permute-start | bytes 80312 | tf_op jit(solution)/shard_map/ppermute | solution.py:268
  226.4 11.1 %collective-permute-start.14 = (f32[8,48,268]{2,1,0:T(8,128)}, f32[8,48,268]{2,1,0:T(8,128)}, u32[]{:S(2)}, u32[]{:S(2)}) collective-permute-start(f32[8,48,268]{2,1,0:T(8,128)} %dynamic-slice_bitcast_fusion.4), channel_id=1, source_target_pairs={{0,2},{2,0},{4,6},{6,4},{8,10},{10,8},{12,14},{14,12},{16,18},{18,... | collective-permute-start | bytes 1234952 | tf_op jit(solution)/shard_map/ppermute | solution.py:268
  226.4 6.5 %collective-permute-start.26 = (f32[6692]{0:T(1024)S(1)}, f32[6692]{0:T(1024)S(1)}, u32[]{:S(2)}, u32[]{:S(2)}) collective-permute-start(f32[6692]{0:T(1024)S(1)} %add.519), channel_id=1, source_target_pairs={{0,16},{2,18},{4,20},{6,22},{8,24},{10,26},{12,28},{14,30},{16,0},... | collective-permute-start | bytes 80312 | tf_op jit(solution)/shard_map/ppermute | solution.py:268
  233.1 3.7 %collective-permute-start.27 = (f32[2048]{0:T(1024)S(1)}, f32[2048]{0:T(1024)S(1)}, u32[]{:S(2)}, u32[]{:S(2)}) collective-permute-start(f32[2048]{0:T(1024)S(1)} %concatenate.17), channel_id=1, source_target_pairs={{0,1},{1,0},{2,3},{3,2},{4,5},{5,4},{6,7},{7,6},{8,9},{9,8},{10,11... | collective-permute-start | bytes 24584 | tf_op jit(solution)/shard_map/ppermute | solution.py:268
  238.8 8.7 %collective-permute-start.15 = (f32[4,48,268]{2,1,0:T(8,128)S(1)}, f32[4,48,268]{2,1,0:T(8,128)S(1)}, u32[]{:S(2)}, u32[]{:S(2)}) collective-permute-start(f32[4,48,268]{2,1,0:T(8,128)S(1)} %dynamic-slice_bitcast_fusion.8), channel_id=1, source_target_pairs={{0,4},{2,6},{4,0},{6,2},{8,12},{10,14},{12,8},{14,10},{16,20},{18,... | collective-permute-start | bytes 617480 | tf_op jit(solution)/shard_map/ppermute | solution.py:268
  247.6 9.3 %collective-permute-start.16 = (f32[2,48,268]{2,1,0:T(8,128)S(1)}, f32[2,48,268]{2,1,0:T(8,128)S(1)}, u32[]{:S(2)}, u32[]{:S(2)}) collective-permute-start(f32[2,48,268]{2,1,0:T(8,128)S(1)} %dynamic-slice_bitcast_fusion.11), channel_id=1, source_target_pairs={{0,8},{2,10},{4,12},{6,14},{8,0},{10,2},{12,4},{14,6},{16,24},{18,... | collective-permute-start | bytes 308744 | tf_op jit(solution)/shard_map/ppermute | solution.py:268
  251.0 16.5 %collective-permute-start.11 = (f32[4,48,768]{2,1,0:T(8,128)}, f32[4,48,768]{2,1,0:T(8,128)}, u32[]{:S(2)}, u32[]{:S(2)}) collective-permute-start(f32[4,48,768]{2,1,0:T(8,128)} %dynamic-slice_bitcast_fusion.5), channel_id=1, source_target_pairs={{0,4},{2,6},{4,0},{6,2},{8,12},{10,14},{12,8},{14,10},{16,20},{18,... | collective-permute-start | bytes 1769480 | tf_op jit(solution)/shard_map/ppermute | solution.py:268
  253.9 26.2 %collective-permute-start.7 = (f32[4,48,768]{2,1,0:T(8,128)}, f32[4,48,768]{2,1,0:T(8,128)}, u32[]{:S(2)}, u32[]{:S(2)}) collective-permute-start(f32[4,48,768]{2,1,0:T(8,128)} %dynamic-slice_bitcast_fusion.6), channel_id=1, source_target_pairs={{0,4},{2,6},{4,0},{6,2},{8,12},{10,14},{12,8},{14,10},{16,20},{18,... | collective-permute-start | bytes 1769480 | tf_op jit(solution)/shard_map/ppermute | solution.py:268
  257.0 5.3 %collective-permute-start.17 = (f32[1,48,268]{2,1,0:T(8,128)S(1)}, f32[1,48,268]{2,1,0:T(8,128)S(1)}, u32[]{:S(2)}, u32[]{:S(2)}) collective-permute-start(f32[1,48,268]{2,1,0:T(8,128)S(1)} %constant_dynamic-slice_fusion.1), channel_id=1, source_target_pairs={{0,16},{2,18},{4,20},{6,22},{8,24},{10,26},{12,28},{14,30},{16,0},... | collective-permute-start | bytes 154376 | tf_op jit(solution)/shard_map/ppermute | solution.py:268
  260.0 30.4 %collective-permute-start.20 = (f32[4,48,768]{2,1,0:T(8,128)}, f32[4,48,768]{2,1,0:T(8,128)}, u32[]{:S(2)}, u32[]{:S(2)}) collective-permute-start(f32[4,48,768]{2,1,0:T(8,128)} %dynamic-slice_bitcast_fusion.3), channel_id=1, source_target_pairs={{0,4},{2,6},{4,0},{6,2},{8,12},{10,14},{12,8},{14,10},{16,20},{18,... | collective-permute-start | bytes 1769480 | tf_op jit(solution)/shard_map/ppermute | solution.py:268
  262.4 4.1 %collective-permute-start.18 = (f32[48,256]{1,0:T(8,128)S(1)}, f32[48,256]{1,0:T(8,128)S(1)}, u32[]{:S(2)}, u32[]{:S(2)}) collective-permute-start(f32[48,256]{1,0:T(8,128)S(1)} %slice.148), channel_id=1, source_target_pairs={{0,1},{1,0},{2,3},{3,2},{4,5},{5,4},{6,7},{7,6},{8,9},{9,8},{10,11... | collective-permute-start | bytes 147464 | tf_op jit(solution)/shard_map/ppermute | solution.py:268
  268.7 24.4 %collective-permute-start.12 = (f32[2,48,768]{2,1,0:T(8,128)S(1)}, f32[2,48,768]{2,1,0:T(8,128)S(1)}, u32[]{:S(2)}, u32[]{:S(2)}) collective-permute-start(f32[2,48,768]{2,1,0:T(8,128)S(1)} %dynamic-slice_bitcast_fusion.9), channel_id=1, source_target_pairs={{0,8},{2,10},{4,12},{6,14},{8,0},{10,2},{12,4},{14,6},{16,24},{18,... | collective-permute-start | bytes 884744 | tf_op jit(solution)/shard_map/ppermute | solution.py:268
  281.5 29.3 %copy-start.32 = (f32[48,2,768]{2,1,0:T(2,128)S(1)}, f32[48,2,768]{2,1,0:T(2,128)}, u32[]{:S(2)}) copy-start(f32[48,2,768]{2,1,0:T(2,128)} %param.31) | copy-start | bytes 884740
  281.5 29.3 %copy-start.39 = (f32[48,2,768]{2,1,0:T(2,128)S(1)}, f32[48,2,768]{2,1,0:T(2,128)}, u32[]{:S(2)}) copy-start(f32[48,2,768]{2,1,0:T(2,128)} %param.40) | copy-start | bytes 884740
  281.5 12.7 %collective-permute-start.8 = (f32[2,48,768]{2,1,0:T(8,128)S(1)}, f32[2,48,768]{2,1,0:T(8,128)S(1)}, u32[]{:S(2)}, u32[]{:S(2)}) collective-permute-start(f32[2,48,768]{2,1,0:T(8,128)S(1)} %dynamic-slice_bitcast_fusion.10), channel_id=1, source_target_pairs={{0,8},{2,10},{4,12},{6,14},{8,0},{10,2},{12,4},{14,6},{16,24},{18,... | collective-permute-start | bytes 884744 | tf_op jit(solution)/shard_map/ppermute | solution.py:268
  291.6 12.3 %collective-permute-start.21 = (f32[2,48,768]{2,1,0:T(8,128)S(1)}, f32[2,48,768]{2,1,0:T(8,128)S(1)}, u32[]{:S(2)}, u32[]{:S(2)}) collective-permute-start(f32[2,48,768]{2,1,0:T(8,128)S(1)} %dynamic-slice_bitcast_fusion.7), channel_id=1, source_target_pairs={{0,8},{2,10},{4,12},{6,14},{8,0},{10,2},{12,4},{14,6},{16,24},{18,... | collective-permute-start | bytes 884744 | tf_op jit(solution)/shard_map/ppermute | solution.py:268
  293.2 10.9 %collective-permute-start.13 = (f32[1,48,768]{2,1,0:T(8,128)S(1)}, f32[1,48,768]{2,1,0:T(8,128)S(1)}, u32[]{:S(2)}, u32[]{:S(2)}) collective-permute-start(f32[1,48,768]{2,1,0:T(8,128)S(1)} %constant_dynamic-slice_fusion.2), channel_id=1, source_target_pairs={{0,16},{2,18},{4,20},{6,22},{8,24},{10,26},{12,28},{14,30},{16,0},... | collective-permute-start | bytes 442376 | tf_op jit(solution)/shard_map/ppermute | solution.py:268
  294.3 16.5 %collective-permute-start.9 = (f32[1,48,768]{2,1,0:T(8,128)S(1)}, f32[1,48,768]{2,1,0:T(8,128)S(1)}, u32[]{:S(2)}, u32[]{:S(2)}) collective-permute-start(f32[1,48,768]{2,1,0:T(8,128)S(1)} %constant_dynamic-slice_fusion.3), channel_id=1, source_target_pairs={{0,16},{2,18},{4,20},{6,22},{8,24},{10,26},{12,28},{14,30},{16,0},... | collective-permute-start | bytes 442376 | tf_op jit(solution)/shard_map/ppermute | solution.py:268
  304.0 10.9 %collective-permute-start.22 = (f32[1,48,768]{2,1,0:T(8,128)S(1)}, f32[1,48,768]{2,1,0:T(8,128)S(1)}, u32[]{:S(2)}, u32[]{:S(2)}) collective-permute-start(f32[1,48,768]{2,1,0:T(8,128)S(1)} %constant_dynamic-slice_fusion), channel_id=1, source_target_pairs={{0,16},{2,18},{4,20},{6,22},{8,24},{10,26},{12,28},{14,30},{16,0},... | collective-permute-start | bytes 442376 | tf_op jit(solution)/shard_map/ppermute | solution.py:268
  (65 other events, 484.6 us)
Sparse Core Ops, SparseCore 0:
  11.9 52.8 all-gather.1
